TPU v7x, 512 devices: a whole 4x4x16 slice. The times are simulated.
512 devices in a mesh: row: 128 (over y, z, core), col: 4 (over x).
Axes of the slice: x: 4, y: 4, z: 16, core: 2. Of those that a mesh axis runs over, the one named last changes fastest.
Arguments:
- residual: float32 [65536, 128], P('row'), may hold values from -6 to 6
- solution: float32 [65536, 128], P('row'), may hold values from -6 to 6
- near_field_blocks: float32 [256, 4, 256, 256], P('row', 'col'), may hold values from -0.09375 to 0.09375
- near_cols: int32 [256, 4], P('row', 'col'), may hold values from 0 to 255, as said below
- couplings: float32 [256, 64, 16, 16], P('row', 'col'), may hold values from -0.1875 to 0.1875
- far_cols: int32 [256, 64], P('row', 'col'), may hold values from 0 to 255, as said below
- far_count: int32 [256], P('row'), may hold values from 16 to 64, as said below
- col_basis: float32 [256, 16, 256], P('row'), may hold values from -0.375 to 0.375
- row_basis: float32 [256, 16, 256], P('row'), may hold values from -0.75 to 0.75
Outputs:
- solution_next: float32 [65536, 128], P('row')
- hessenberg: float32 [5, 4, 128], replicated
Inputs may be any that keep to these rules, and one draw needn't show every extreme that they name: near_cols[i, 0] = i; the other entries of row cluster i are i + t for distinct nonzero t with |t| <= 2, clipped to 0 .. 255. far_cols[i, p] differs from i by more than 2, counted around the ends of the cluster range. Slots p >= far_count[i] of row cluster i are unused; some row cluster uses all 64 slots.
All inputs are finite; a program needn't handle non-finite values.
Results may differ from a plain program's by a relative error of at most 0.0001.
Values sent between devices are 32-bit elements; how exact they have to be, the bound alone decides.
A program may use at most 64 MiB of HBM per device.

v0:
```python
import jax
import jax.numpy as jnp
from jax import lax
from jax.sharding import PartitionSpec as P

LEAF_UNKNOWNS = 256
CL_DEV = 2
REACH = 2
SB = 4
HIGH = lax.Precision.HIGHEST
SHIFT = 1.0


def with_halo(value, sides, width):
    for axis, dim in sides:
        peers, length = (lax.axis_size(axis), value.shape[dim])
        up = [(i, (i + 1) % peers) for i in range(peers - 1)]
        down = [(j, i) for i, j in up]
        last = lax.slice_in_dim(value, length - width, length, axis=dim)
        first = lax.slice_in_dim(value, 0, width, axis=dim)
        before = lax.ppermute(last, axis, up)
        after = lax.ppermute(first, axis, down)
        value = jnp.concatenate([before, value, after], axis=dim)
    return value


def cholesky_upper(entries, order_n):
    zero_entry = jnp.zeros_like(entries[0][0])
    upper_r = []
    for row_idx in range(order_n):
        upper_r.append([zero_entry] * order_n)
    for row_idx in range(order_n):
        running = entries[row_idx][row_idx]
        for earlier in range(row_idx):
            running = running - upper_r[earlier][row_idx] * upper_r[earlier][row_idx]
        pivot_val = jnp.sqrt(running)
        upper_r[row_idx][row_idx] = pivot_val
        for col_idx in range(row_idx + 1, order_n):
            entry_val = entries[row_idx][col_idx]
            for earlier in range(row_idx):
                entry_val = entry_val - upper_r[earlier][row_idx] * upper_r[earlier][col_idx]
            upper_r[row_idx][col_idx] = entry_val / pivot_val
    return upper_r


def small_update(gram_sum, scale_factor, depth_n):
    order_n = depth_n + 1
    entries = [
        [gram_sum[row_idx, col_idx] for col_idx in range(order_n)] for row_idx in range(order_n)
    ]
    upper_r = cholesky_upper(entries, order_n)
    shifted = [
        [
            SHIFT * upper_r[row_idx][col_idx] + upper_r[row_idx][col_idx + 1]
            for col_idx in range(depth_n)
        ]
        for row_idx in range(order_n)
    ]
    hessen = []
    for row_idx in range(order_n):
        row_vals = []
        for col_idx in range(depth_n):
            entry_val = shifted[row_idx][col_idx]
            for earlier in range(col_idx):
                entry_val = entry_val - row_vals[earlier] * upper_r[earlier][col_idx]
            row_vals.append(entry_val / upper_r[col_idx][col_idx])
        hessen.append(row_vals)
    normal = []
    for row_idx in range(depth_n):
        row_vals = []
        for col_idx in range(depth_n):
            entry_val = hessen[0][row_idx] * hessen[0][col_idx]
            for inner in range(1, order_n):
                entry_val = entry_val + hessen[inner][row_idx] * hessen[inner][col_idx]
            row_vals.append(entry_val)
        normal.append(row_vals)
    target = [scale_factor * upper_r[0][0] * hessen[0][col_idx] for col_idx in range(depth_n)]
    factor = cholesky_upper(normal, depth_n)
    forward = []
    for row_idx in range(depth_n):
        entry_val = target[row_idx]
        for earlier in range(row_idx):
            entry_val = entry_val - factor[earlier][row_idx] * forward[earlier]
        forward.append(entry_val / factor[row_idx][row_idx])
    solved = [None] * depth_n
    for row_idx in range(depth_n - 1, -1, -1):
        entry_val = forward[row_idx]
        for later in range(row_idx + 1, depth_n):
            entry_val = entry_val - factor[row_idx][later] * solved[later]
        solved[row_idx] = entry_val / factor[row_idx][row_idx]
    weights = [None] * depth_n
    for row_idx in range(depth_n - 1, -1, -1):
        entry_val = solved[row_idx]
        for later in range(row_idx + 1, depth_n):
            entry_val = entry_val - upper_r[row_idx][later] * weights[later]
        weights[row_idx] = entry_val / upper_r[row_idx][row_idx]
    hess_array = jnp.stack([jnp.stack(hessen[row_idx], 0) for row_idx in range(order_n)], 0)
    return (hess_array, weights)


def local(
    residual,
    solution,
    near_field_blocks,
    near_cols,
    couplings,
    far_cols,
    far_count,
    col_basis,
    row_basis,
):
    first_cluster = lax.axis_index("row") * CL_DEV
    blocks, couple = (near_field_blocks, couplings)
    near_idx, far_idx = (near_cols, far_cols)
    positions = lax.axis_index("col") * couplings.shape[1] + jnp.arange(
        couplings.shape[1], dtype=jnp.int32
    )
    live_mask = (positions[None, :] < far_count[:, None]).astype(jnp.float32)
    weighted = couple * live_mask[:, :, None, None]
    local_near = near_idx - (first_cluster - REACH)
    scale_factor = jnp.ones((residual.shape[1],), jnp.float32)
    current = residual
    basis_list = [current]
    for step_k in range(SB):
        width_r = current.shape[1]
        extended = with_halo(current, (("row", 0),), REACH * LEAF_UNKNOWNS)
        panels = extended.reshape(CL_DEV + 2 * REACH, LEAF_UNKNOWNS, width_r)
        picked = jnp.take(panels, local_near, axis=0)
        near_part = jnp.einsum("csab,csbr->car", blocks, picked, precision=HIGH)
        own_panels = current.reshape(CL_DEV, LEAF_UNKNOWNS, width_r)
        coeffs = jnp.einsum("ckb,cbr->ckr", col_basis, own_panels, precision=HIGH)
        table = lax.all_gather(coeffs, "row", axis=0, tiled=True)
        fetched = jnp.take(table, far_idx, axis=0)
        summed = jnp.einsum("cfkl,cflr->ckr", weighted, fetched, precision=HIGH)
        far_part = jnp.einsum("ckb,ckr->cbr", row_basis, summed, precision=HIGH)
        partial_value = (near_part + far_part).reshape(CL_DEV * LEAF_UNKNOWNS, width_r)
        current = lax.psum(partial_value, "col")
        basis_list.append(current)
    stacked = jnp.stack(basis_list, 0)
    local_gram = jnp.einsum("anr,bnr->abr", stacked, stacked, precision=HIGH)
    gram_sum = lax.psum(local_gram, "row")
    hessenberg, weights = small_update(gram_sum, scale_factor, SB)
    new_sol = solution
    for step_k in range(SB):
        new_sol = new_sol + weights[step_k][None, :] * basis_list[step_k]
    return (new_sol, hessenberg)


def solution(mesh):
    placed = (
        P("row", None),
        P("row", None),
        P("row", "col", None, None),
        P("row", "col"),
        P("row", "col", None, None),
        P("row", "col"),
        P("row"),
        P("row", None, None),
        P("row", None, None),
    )
    return jax.shard_map(
        local, mesh=mesh, in_specs=placed, out_specs=(P("row", None), P()), check_vma=False
    )
```

profile of v0, /device:TPU:4, one launch (start us, length us, event | category | flops | bytes accessed | tf_op | source)
XLA Modules:
  0.0 1346.1 jit_solution(8567163214037070050)
XLA Ops:
  7.2 1.9 fusion.85
  9.2 1.8 collective-permute-start
  14.5 1.8 collective-permute-done.1
  17.9 139.1 %all-gather.5.cloned.1.call-done = f32[256,16,128]{2,1,0:T(8,128)} async-done(((f32[2,16,128]{2,1,0:T(8,128)}), f32[256,16,128]{2,1,0:T(8,128)}) %all-gather.5.cloned.1.call-update) | async-done | bytes 2097168 | tf_op jit(solution)/shard_map/all_gather | solution.py:132
  157.0 2.2 gather_fusion.1
  162.2 52.8 %all-reduce.5.cloned.1.call-done = f32[512,128]{0,1:T(8,128)} async-done(((f32[512,128]{0,1:T(8,128)}), f32[512,128]{0,1:T(8,128)}) %all-reduce.5.cloned.1.call-update) | async-done | bytes 262160 | tf_op jit(solution)/shard_map/psum | solution.py:137
  217.1 1.3 collective-permute-start.2
  219.7 4.1 collective-permute-done.3
  225.7 135.3 %all-gather.7.cloned.1.call-done = f32[256,16,128]{2,1,0:T(8,128)} async-done(((f32[2,16,128]{2,1,0:T(8,128)}), f32[256,16,128]{2,1,0:T(8,128)}) %all-gather.7.cloned.1.call-update) | async-done | bytes 2097168 | tf_op jit(solution)/shard_map/all_gather | solution.py:132
  360.9 2.2 gather_fusion.3
  366.2 52.8 %all-reduce.7.cloned.1.call-done = f32[512,128]{0,1:T(8,128)} async-done(((f32[512,128]{0,1:T(8,128)}), f32[512,128]{0,1:T(8,128)}) %all-reduce.7.cloned.1.call-update) | async-done | bytes 262160 | tf_op jit(solution)/shard_map/psum | solution.py:137
  423.6 4.1 collective-permute-done.5
  429.6 135.1 %all-gather.9.cloned.1.call-done = f32[256,16,128]{2,1,0:T(8,128)} async-done(((f32[2,16,128]{2,1,0:T(8,128)}), f32[256,16,128]{2,1,0:T(8,128)}) %all-gather.9.cloned.1.call-update) | async-done | bytes 2097168 | tf_op jit(solution)/shard_map/all_gather | solution.py:132
  564.7 2.2 gather_fusion.5
  569.9 52.8 %all-reduce.9.cloned.1.call-done = f32[512,128]{0,1:T(8,128)} async-done(((f32[512,128]{0,1:T(8,128)}), f32[512,128]{0,1:T(8,128)}) %all-reduce.9.cloned.1.call-update) | async-done | bytes 262160 | tf_op jit(solution)/shard_map/psum | solution.py:137
  626.1 1.5 collective-permute-start.7
  627.6 3.9 collective-permute-done.7
  633.4 135.3 %all-gather.11.cloned.1.call-done = f32[256,16,128]{2,1,0:T(8,128)} async-done(((f32[2,16,128]{2,1,0:T(8,128)}), f32[256,16,128]{2,1,0:T(8,128)}) %all-gather.11.cloned.1.call-update) | async-done | bytes 2097168 | tf_op jit(solution)/shard_map/all_gather | solution.py:132
  768.6 2.2 gather_fusion.7
  779.2 47.4 %all-reduce.11.cloned.1.call-done = f32[1,512,128]{1,0,2:T(1,128)} async-done(((f32[1,512,128]{1,0,2:T(1,128)}), f32[1,512,128]{1,0,2:T(1,128)}) %all-reduce.11.cloned.1.call-update) | async-done | bytes 262160 | tf_op jit(solution)/shard_map/psum | solution.py:137
  826.6 4.6 stack.76
  831.2 3.7 convolution_bitcast_fusion
  834.9 495.3 %psum.39 = f32[5,5,128]{0,1,2:T(8,128)S(1)} all-reduce(f32[5,5,128]{0,1,2:T(8,128)} %convolution_bitcast_fusion), channel_id=1, replica_groups=mesh['row'=128,'col'=4] {'row'}, use_global_device_ids=true, to_apply=%region_4.7 | all-reduce | flops 3200 | bytes 25600 | tf_op jit(solution)/shard_map/psum | solution.py:141
  1330.2 6.9 multiply_reduce_fusion
  (115 shorter events, 41.4 us)
Async XLA Ops:
  7.2 153.2 %copy-start = (f32[2,1,256,256]{3,2,1,0:T(8,128)S(1)}, f32[2,1,256,256]{3,2,1,0:T(8,128)}, u32[]{:S(2)}) copy-start(f32[2,1,256,256]{3,2,1,0:T(8,128)} %param.15) | copy-start | bytes 1572868
  7.2 152.0 %copy-start.1 = (f32[2,16,16,16]{3,2,1,0:T(8,128)S(1)}, f32[2,16,16,16]{3,2,1,0:T(8,128)}, u32[]{:S(2)}) copy-start(f32[2,16,16,16]{3,2,1,0:T(8,128)} %param.17) | copy-start | bytes 98308
  7.2 152.7 %copy-start.9 = (f32[2,16,256]{2,1,0:T(8,128)S(1)}, f32[2,16,256]{2,1,0:T(8,128)}, u32[]{:S(2)}) copy-start(f32[2,16,256]{2,1,0:T(8,128)} %param.21) | copy-start | bytes 98308
  7.2 149.8 %all-gather.5.cloned.1.call-start = ((), (), s32[]{:S(2)}) async-start(), calls=%async_computation | async-start | bytes 2113536 | tf_op jit(solution)/shard_map/all_gather | solution.py:132
  9.2 205.9 %all-reduce.5.cloned.1.call-start = ((), (), s32[]{:S(2)}) async-start(), calls=%async_computation.1 | async-start | bytes 524288 | tf_op jit(solution)/shard_map/psum | solution.py:137
  9.2 5.3 collective-permute-start
  11.0 5.3 collective-permute-start.1
  159.1 57.0 %copy-start.8 = (f32[2,16,256]{2,1,0:T(8,128)S(1)}, f32[2,16,256]{2,1,0:T(8,128)}, u32[]{:S(2)}) copy-start(f32[2,16,256]{2,1,0:T(8,128)} %param.20) | copy-start | bytes 98308
  162.2 198.8 %all-gather.7.cloned.1.call-start = ((), (), s32[]{:S(2)}) async-start(), calls=%async_computation.2 | async-start | bytes 2113536 | tf_op jit(solution)/shard_map/all_gather | solution.py:132
  217.0 201.9 %all-reduce.7.cloned.1.call-start = ((), (), s32[]{:S(2)}) async-start(), calls=%async_computation.3 | async-start | bytes 524288 | tf_op jit(solution)/shard_map/psum | solution.py:137
  217.1 2.7 collective-permute-start.2
  218.4 5.4 collective-permute-start.3
  366.1 198.6 %all-gather.9.cloned.1.call-start = ((), (), s32[]{:S(2)}) async-start(), calls=%async_computation.4 | async-start | bytes 2113536 | tf_op jit(solution)/shard_map/all_gather | solution.py:132
  420.9 201.8 %all-reduce.9.cloned.1.call-start = ((), (), s32[]{:S(2)}) async-start(), calls=%async_computation.5 | async-start | bytes 524288 | tf_op jit(solution)/shard_map/psum | solution.py:137
  421.0 2.7 collective-permute-start.4
  422.3 5.4 collective-permute-start.5
  569.9 198.7 %all-gather.11.cloned.1.call-start = ((), (), s32[]{:S(2)}) async-start(), calls=%async_computation.6 | async-start | bytes 2113536 | tf_op jit(solution)/shard_map/all_gather | solution.py:132
  624.7 201.9 %all-reduce.11.cloned.1.call-start = ((), (), s32[]{:S(2)}) async-start(), calls=%async_computation.7 | async-start | bytes 524288 | tf_op jit(solution)/shard_map/psum | solution.py:137
  624.8 2.8 collective-permute-start.6
  626.1 5.4 collective-permute-start.7
  633.3 140.5 %copy-start.2 = (f32[512,128]{1,0:T(8,128)S(1)}, f32[512,128]{1,0:T(8,128)}, u32[]{:S(2)}) copy-start(f32[512,128]{1,0:T(8,128)} %param.13) | copy-start | bytes 786436
  772.8 5.5 copy-start.5
  834.9 502.6 %copy-start.6 = (f32[512,128]{0,1:T(8,128)S(1)}, f32[512,128]{0,1:T(8,128)}, u32[]{:S(2)}) copy-start(f32[512,128]{0,1:T(8,128)} %copy.65) | copy-start | bytes 786436
  834.9 502.6 %copy-start.7 = (f32[512,128]{0,1:T(8,128)S(1)}, f32[512,128]{0,1:T(8,128)}, u32[]{:S(2)}) copy-start(f32[512,128]{0,1:T(8,128)} %copy.66) | copy-start | bytes 786436
  (4 other events, 14.2 us)
Sparse Core Ops, SparseCore 0:
  11.7 145.1 all-gather.4
  162.3 52.7 all-reduce.4
  218.8 142.1 all-gather.6
  366.2 52.6 all-reduce.6
  422.5 142.1 all-gather.8
  570.0 52.7 all-reduce.8
  626.5 142.1 all-gather.10
  773.9 52.6 all-reduce.10
where the time goes:
time: 1350 us
  waiting for transfers between devices  765 us (57%)
  blocking collectives  495 us (37%)
  local copies, waits for them, and re-layouts  30.2 us (2%)
  matrix products  16.2 us (1%)
  between operations  14.7 us (1%)
  other arithmetic  13.6 us (1%)
    all_gather x4, waiting for transfers between devices, local(): table = lax.all_gather(coeffs, 'row', axis=0, tiled=True)  545 us
    psum x1, blocking collectives, local(): gram_sum = lax.psum(local_gram, 'row')  495 us
    psum x4, waiting for transfers between devices, local(): current = lax.psum(partial_value, 'col')  206 us
  transfers between devices with their start and end apart: 16, of which 12 were waited for; matrix products, arithmetic and copies ran while one was open for 1% of the time, Pallas kernels for 0%

commit v1 on v0

--- a/solution.py
+++ b/solution.py
@@ -138,7 +138,7 @@
         basis_list.append(current)
     stacked = jnp.stack(basis_list, 0)
     local_gram = jnp.einsum("anr,bnr->abr", stacked, stacked, precision=HIGH)
-    gram_sum = lax.psum(local_gram, "row")
+    gram_sum = jnp.sum(lax.all_gather(local_gram, "row"), axis=0)
     hessenberg, weights = small_update(gram_sum, scale_factor, SB)
     new_sol = solution
     for step_k in range(SB):

time: 1350 us -> 993 us (0.74)
  the two profiles are of different devices: /device:TPU:4 before, /device:TPU:1 now
where the time goes in v1:
time: 993 us; the launch traced here: 991 us
  waiting for transfers between devices  887 us (89%)
  starting transfers between devices  34 us (3%)
  local copies, waits for them, and re-layouts  31.6 us (3%)
  matrix products  16.2 us (2%)
  between operations  14.4 us (1%)
    all_gather x4, waiting for transfers between devices, local(): table = lax.all_gather(coeffs, 'row', axis=0, tiled=True)  524 us
    psum x4, waiting for transfers between devices, local(): current = lax.psum(partial_value, 'col')  201 us
    all_gather x1, waiting for transfers between devices, local(): gram_sum = jnp.sum(lax.all_gather(local_gram, 'row'), axis=0)  143 us
    ppermute x4, starting transfers between devices, with_halo(): before = lax.ppermute(last, axis, up)  22.5 us
  transfers between devices with their start and end apart: 17, of which 16 were waited for; matrix products, arithmetic and copies ran while one was open for 1% of the time, Pallas kernels for 0%

profile of v1, /device:TPU:1, one launch (start us, length us, event | category | flops | bytes accessed | tf_op | source)
XLA Modules:
  0.0 991.4 jit_solution(2834541090725968151)
XLA Ops:
  9.2 4.9 collective-permute-start
  14.1 5.1 collective-permute-start.1
  23.6 134.6 %all-gather.7.cloned.1.call-done = f32[256,16,128]{2,1,0:T(8,128)} async-done(((f32[2,16,128]{2,1,0:T(8,128)}), f32[256,16,128]{2,1,0:T(8,128)}) %all-gather.7.cloned.1.call-update) | async-done | bytes 2097168 | tf_op jit(solution)/shard_map/all_gather | solution.py:132
  158.2 2.2 gather_fusion.1
  163.4 51.1 %all-reduce.5.cloned.1.call-done = f32[512,128]{0,1:T(8,128)} async-done(((f32[512,128]{0,1:T(8,128)}), f32[512,128]{0,1:T(8,128)}) %all-reduce.5.cloned.1.call-update) | async-done | bytes 262160 | tf_op jit(solution)/shard_map/psum | solution.py:137
  216.6 5.9 collective-permute-start.2
  226.1 4.3 collective-permute-done.3
  232.2 129.9 %all-gather.9.cloned.1.call-done = f32[256,16,128]{2,1,0:T(8,128)} async-done(((f32[2,16,128]{2,1,0:T(8,128)}), f32[256,16,128]{2,1,0:T(8,128)}) %all-gather.9.cloned.1.call-update) | async-done | bytes 2097168 | tf_op jit(solution)/shard_map/all_gather | solution.py:132
  362.2 2.2 gather_fusion.3
  367.4 51.1 %all-reduce.7.cloned.1.call-done = f32[512,128]{0,1:T(8,128)} async-done(((f32[512,128]{0,1:T(8,128)}), f32[512,128]{0,1:T(8,128)}) %all-reduce.7.cloned.1.call-update) | async-done | bytes 262160 | tf_op jit(solution)/shard_map/psum | solution.py:137
  420.5 5.9 collective-permute-start.4
  430.0 4.3 collective-permute-done.5
  436.2 129.8 %all-gather.11.cloned.1.call-done = f32[256,16,128]{2,1,0:T(8,128)} async-done(((f32[2,16,128]{2,1,0:T(8,128)}), f32[256,16,128]{2,1,0:T(8,128)}) %all-gather.11.cloned.1.call-update) | async-done | bytes 2097168 | tf_op jit(solution)/shard_map/all_gather | solution.py:132
  565.9 2.2 gather_fusion.5
  571.2 51.1 %all-reduce.9.cloned.1.call-done = f32[512,128]{0,1:T(8,128)} async-done(((f32[512,128]{0,1:T(8,128)}), f32[512,128]{0,1:T(8,128)}) %all-reduce.9.cloned.1.call-update) | async-done | bytes 262160 | tf_op jit(solution)/shard_map/psum | solution.py:137
  624.3 5.9 collective-permute-start.6
  633.8 4.3 collective-permute-done.7
  640.0 129.9 %all-gather.13.cloned.1.call-done = f32[256,16,128]{2,1,0:T(8,128)} async-done(((f32[2,16,128]{2,1,0:T(8,128)}), f32[256,16,128]{2,1,0:T(8,128)}) %all-gather.13.cloned.1.call-update) | async-done | bytes 2097168 | tf_op jit(solution)/shard_map/all_gather | solution.py:132
  769.9 2.2 gather_fusion.7
  779.0 47.2 %all-reduce.11.cloned.1.call-done = f32[1,512,128]{1,0,2:T(1,128)} async-done(((f32[1,512,128]{1,0,2:T(1,128)}), f32[1,512,128]{1,0,2:T(1,128)}) %all-reduce.11.cloned.1.call-update) | async-done | bytes 262160 | tf_op jit(solution)/shard_map/psum | solution.py:137
  826.2 4.6 stack.76
  830.8 3.7 convolution_bitcast_fusion
  837.6 143.2 %all-gather.15.cloned.1.call-done = f32[640,5,128]{2,1,0:T(8,128)} async-done(((f32[5,5,128]{2,1,0:T(8,128)}), f32[640,5,128]{2,1,0:T(8,128)}) %all-gather.15.cloned.1.call-update) | async-done | bytes 1638416 | tf_op jit(solution)/shard_map/all_gather | solution.py:141
  980.7 2.0 reduce_sum.9
  (116 shorter events, 49.7 us)
Async XLA Ops:
  7.2 154.4 %copy-start = (f32[2,1,256,256]{3,2,1,0:T(8,128)S(1)}, f32[2,1,256,256]{3,2,1,0:T(8,128)}, u32[]{:S(2)}) copy-start(f32[2,1,256,256]{3,2,1,0:T(8,128)} %param.15) | copy-start | bytes 1572868
  7.2 153.2 %copy-start.1 = (f32[2,16,16,16]{3,2,1,0:T(8,128)S(1)}, f32[2,16,16,16]{3,2,1,0:T(8,128)}, u32[]{:S(2)}) copy-start(f32[2,16,16,16]{3,2,1,0:T(8,128)} %param.17) | copy-start | bytes 98308
  7.2 154.0 %copy-start.8 = (f32[2,16,256]{2,1,0:T(8,128)S(1)}, f32[2,16,256]{2,1,0:T(8,128)}, u32[]{:S(2)}) copy-start(f32[2,16,256]{2,1,0:T(8,128)} %param.21) | copy-start | bytes 98308
  7.2 151.0 %all-gather.7.cloned.1.call-start = ((), (), s32[]{:S(2)}) async-start(), calls=%async_computation | async-start | bytes 2113536 | tf_op jit(solution)/shard_map/all_gather | solution.py:132
  9.2 205.4 %all-reduce.5.cloned.1.call-start = ((), (), s32[]{:S(2)}) async-start(), calls=%async_computation.1 | async-start | bytes 524288 | tf_op jit(solution)/shard_map/psum | solution.py:137
  9.2 12.3 %collective-permute-start = (f32[512,128]{1,0:T(8,128)}, f32[512,128]{1,0:T(8,128)S(1)}, u32[]{:S(2)}, u32[]{:S(2)}) collective-permute-start(f32[512,128]{1,0:T(8,128)} %param.13), channel_id=1, source_target_pairs={{0,4},{4,8},{8,12},{12,16},{16,20},{20,24},{24,28},{28,32},{32,36}... | collective-permute-start | bytes 786440 | tf_op jit(solution)/shard_map/ppermute | solution.py:21
  14.1 7.9 collective-permute-start.1
  160.4 55.3 %copy-start.7 = (f32[2,16,256]{2,1,0:T(8,128)S(1)}, f32[2,16,256]{2,1,0:T(8,128)}, u32[]{:S(2)}) copy-start(f32[2,16,256]{2,1,0:T(8,128)} %param.20) | copy-start | bytes 98308
  163.4 198.8 %all-gather.9.cloned.1.call-start = ((), (), s32[]{:S(2)}) async-start(), calls=%async_computation.2 | async-start | bytes 2113536 | tf_op jit(solution)/shard_map/all_gather | solution.py:132
  216.5 202.0 %all-reduce.7.cloned.1.call-start = ((), (), s32[]{:S(2)}) async-start(), calls=%async_computation.3 | async-start | bytes 524288 | tf_op jit(solution)/shard_map/psum | solution.py:137
  216.6 9.5 collective-permute-start.2
  222.5 7.9 collective-permute-start.3
  367.3 198.6 %all-gather.11.cloned.1.call-start = ((), (), s32[]{:S(2)}) async-start(), calls=%async_computation.4 | async-start | bytes 2113536 | tf_op jit(solution)/shard_map/all_gather | solution.py:132
  420.5 201.8 %all-reduce.9.cloned.1.call-start = ((), (), s32[]{:S(2)}) async-start(), calls=%async_computation.5 | async-start | bytes 524288 | tf_op jit(solution)/shard_map/psum | solution.py:137
  420.5 9.5 collective-permute-start.4
  426.4 7.9 collective-permute-start.5
  571.1 198.8 %all-gather.13.cloned.1.call-start = ((), (), s32[]{:S(2)}) async-start(), calls=%async_computation.6 | async-start | bytes 2113536 | tf_op jit(solution)/shard_map/all_gather | solution.py:132
  624.3 202.0 %all-reduce.11.cloned.1.call-start = ((), (), s32[]{:S(2)}) async-start(), calls=%async_computation.7 | async-start | bytes 524288 | tf_op jit(solution)/shard_map/psum | solution.py:137
  624.3 9.5 collective-permute-start.6
  630.2 7.9 collective-permute-start.7
  639.9 135.3 %copy-start.2 = (f32[512,128]{1,0:T(8,128)S(1)}, f32[512,128]{1,0:T(8,128)}, u32[]{:S(2)}) copy-start(f32[512,128]{1,0:T(8,128)} %param.13) | copy-start | bytes 786436
  773.3 4.8 copy-start.5
  775.0 205.7 %all-gather.15.cloned.1.call-start = ((), (), s32[]{:S(2)}) async-start(), calls=%async_computation.8 | async-start | bytes 2641920 | tf_op jit(solution)/shard_map/all_gather | solution.py:141
  836.3 146.8 %copy-start.6 = (f32[512,128]{0,1:T(8,128)S(1)}, f32[512,128]{0,1:T(8,128)}, u32[]{:S(2)}) copy-start(f32[512,128]{0,1:T(8,128)} %all-reduce.9.cloned.1.call-done) | copy-start | bytes 786436
  (3 other events, 9.0 us)
Sparse Core Ops, SparseCore 0:
  11.7 146.4 all-gather.6
  163.5 51.0 all-reduce.4
  218.3 143.8 all-gather.8
  367.5 51.0 all-reduce.6
  422.1 143.8 all-gather.10
  571.2 51.0 all-reduce.8
  626.0 143.8 all-gather.12
  775.2 50.9 all-reduce.10
  836.5 144.2 all-gather.14
